TPU v7x, 512 devices: a whole 4x8x8 slice. The times are simulated.
512 devices in a mesh: region: 4 (over z_lo), group: 16 (over z_hi, y), loop: 8 (over x, core).
Axes of the slice: x: 4, y: 8, z: 8 (z_hi: 2, z_lo: 4; z = z_hi * 4 + z_lo), core: 2. Of those that a mesh axis runs over, the one named last changes fastest.
Arguments:
- history: float32 [16, 262144], P(None, ('region', 'group', 'loop')), may hold values from -6 to 6
- incident: float32 [4, 262144], P(None, ('region', 'group', 'loop')), may hold values from -6 to 6
- positions: float32 [3, 262144], P(None, ('region', 'group', 'loop')), may hold values from -1 to 1
- area: float32 [262144], P(('region', 'group', 'loop')), may hold values from 0.00390625 to 0.03125
- self_weight: float32 [262144], P(('region', 'group', 'loop')), may hold values from 1 to 2
- pair_target: int32 [512, 24], P(('region', 'group', 'loop')), may hold values from 0 to 31
- pair_source: int32 [512, 24], P(('region', 'group', 'loop')), may hold values from 0 to 7
- pair_lag: int32 [512, 24], P(('region', 'group', 'loop')), may hold values from 1 to 12
- pair_count: int32 [512], P(('region', 'group', 'loop')), may hold values from 16 to 24, as said below
- junc_send: int32 [512, 128], P(('region', 'group', 'loop')), may hold values from 0 to 511
- junc_recv: int32 [512, 128], P(('region', 'group', 'loop')), may hold values from 0 to 511
- junc_gain: float32 [512, 128], P(('region', 'group', 'loop')), may hold values from 0.5 to 2
- adjacency: int32 [512], P(('region', 'group', 'loop')), may hold values from 1 to 3
Outputs:
- density: float32 [4, 262144], P(None, ('region', 'group', 'loop'))
Inputs may be any that keep to these rules, and one draw needn't show every extreme that they name: `pair_count`: each device uses between 16 and 24 of its listed pairs, and some device uses all 24.
All inputs are finite; a program needn't handle non-finite values.
Results may differ from a plain program's by a relative error of at most 0.0003.
Values sent between devices are 32-bit elements; how exact they have to be, the bound alone decides.
No kernel may reach another device: no remote copies, remote signals or barrier semaphores. Data moves between devices by JAX's collectives and lax.ppermute only.
A program may use at most 64 MiB of HBM per device.

v0:
```python
import functools

import jax
import jax.numpy as jnp
from jax import lax
from jax.experimental import pallas as pl
from jax.experimental.pallas import tpu as pltpu
from jax.sharding import PartitionSpec as P


HIST = 16
STEPS = 4
LANES = 128
SUBS = 8
SOFTEN = 0.25
AREA_ROW = 3
STORED_ROW = 4
FIRST_STORED = 1
COEFS = 4


PAIR_GRANT = pltpu.CompilerParams(vmem_limit_bytes=12 * 2**20)
SMALL_GRANT = pltpu.CompilerParams(vmem_limit_bytes=4 * 2**20)
VMEM = pl.BlockSpec(memory_space=pltpu.VMEM)
SMEM = pl.BlockSpec(memory_space=pltpu.SMEM)


def spline_coefs(rows, scale):
    d, c, b, a = rows
    return (
        (b + 4.0 * c + d) * scale,
        3.0 * (b - d) * scale,
        3.0 * (b - 2.0 * c + d) * scale,
        (a - d + 3.0 * (c - b)) * scale,
    )


def spread_targets(tgt_ref, tile, tb_ref):
    group, start = tile // 2, (tile % 2) * (2 * LANES)
    for k in range(3):
        for b in range(2):
            row = tgt_ref[group, k : k + 1, pl.ds(pl.multiple_of(start + b * LANES, LANES), LANES)]
            tb_ref[k, b * LANES : (b + 1) * LANES, :] = jnp.transpose(jnp.broadcast_to(row, (LANES, LANES)), (1, 0))


def pair_sums(steps, nodes, tb_ref, geo_ref, coef_ref, acc_ref):
    def block_fn(i, carry):
        rows = pl.ds(pl.multiple_of(i * SUBS, SUBS), SUBS)
        coords = [tb_ref[k, rows, :] for k in range(3)]
        sums = [None] * steps
        for c in range(nodes // LANES):
            cols = slice(c * LANES, (c + 1) * LANES)
            dist_sq = None
            for k in range(3):
                delta = coords[k] - geo_ref[k, :, cols]
                square = delta * delta
                dist_sq = square if dist_sq is None else dist_sq + square
            weight = lax.rsqrt(dist_sq + SOFTEN)
            u = 1.0 / (1.0 + dist_sq)
            for n in range(steps):
                mix = coef_ref[n * COEFS + 3, :, cols]
                for power in (2, 1, 0):
                    mix = mix * u + coef_ref[n * COEFS + power, :, cols]
                term = weight * mix
                sums[n] = term if sums[n] is None else sums[n] + term
        for n in range(steps):
            acc_ref[n, rows, :] = sums[n]
        return carry

    lax.fori_loop(0, acc_ref.shape[1] // SUBS, block_fn, 0, unroll=acc_ref.shape[1] // SUBS)


def lane_totals(acc_ref, n):
    return [
        jnp.sum(jnp.transpose(acc_ref[n, b * LANES : (b + 1) * LANES, :], (1, 0)), axis=0, keepdims=True)
        for b in range(2)
    ]


def spread(ref, index, lines):
    for c in range(lines.shape[0]):
        ref[index, :, c * LANES : (c + 1) * LANES] = jnp.broadcast_to(lines[c : c + 1, :], (SUBS, LANES))


def order_kernel(count_ref, lag_ref, order_ref):
    pairs, count = lag_ref.shape[1], count_ref[0]
    lags = [jnp.where(p < count, lag_ref[0, p], 0) for p in range(pairs)]
    filled = jnp.int32(0)
    ends = []
    for lag in range(1, STEPS):
        for p in range(pairs):
            order_ref[filled] = p
            filled = filled + (lags[p] == lag).astype(jnp.int32)
        ends.append(filled)
    for place, end in enumerate(ends + [count]):
        order_ref[pairs + place] = end


def two_at_a_time(count, pick, lists, tgt_ref, src_ref, works, steps, window_of, add):
    target_ref, source_ref, lag_ref = lists
    nodes = src_ref.shape[2] * LANES

    def turn_fn(turn, carry):
        tiles = []
        for side, (tb, geo, coef, acc) in enumerate(works):
            place = 2 * turn + side
            p = pick(jnp.minimum(place, count - 1))
            tile, member, lag = target_ref[0, p], source_ref[0, p], lag_ref[0, p]
            factor = jnp.where(place < count, 1.0 / 6.0, 0.0)
            spread_targets(tgt_ref, tile, tb)
            for k in range(3):
                spread(geo, k, src_ref[member, k])
            scale = src_ref[member, AREA_ROW] * factor
            window = window_of(member, lag)
            for n in range(steps):
                for power, value in enumerate(spline_coefs(window[n : n + 4], scale)):
                    spread(coef, n * COEFS + power, value)
            pair_sums(steps, nodes, tb, geo, coef, acc)
            tiles.append(tile)
        for tile, (_, _, _, acc) in zip(tiles, works):
            add(tile, jnp.concatenate([row for n in range(steps) for row in lane_totals(acc, n)], axis=0))
        return carry

    lax.fori_loop(0, (count + 1) // 2, turn_fn, 0)


def history_kernel(order_ref, target_ref, source_ref, lag_ref, tgt_ref, src_ref, out_ref, *work):
    out_ref[...] = jnp.zeros_like(out_ref)

    def window_of(member, lag):
        first, end = STORED_ROW - FIRST_STORED + HIST - 3 - lag, src_ref.shape[1]
        rows = [src_ref[member, first + i] for i in range(4)]
        for i in range(4, STEPS + 3):
            row = src_ref[member, jnp.minimum(first + i, end - 1)]
            rows.append(jnp.where(first + i < end, row, 0.0))
        return rows

    def add(tile, rows):
        out_ref[tile] += rows

    lists = (target_ref, source_ref, lag_ref)
    two_at_a_time(
        order_ref[target_ref.shape[1] + STEPS - 1], lambda p: p, lists, tgt_ref, src_ref, (work[:4], work[4:]), STEPS, window_of, add
    )


def thirds(row):
    high = row.astype(jnp.bfloat16)
    rest = row - high.astype(jnp.float32)
    middle = rest.astype(jnp.bfloat16)
    low = (rest - middle.astype(jnp.float32)).astype(jnp.bfloat16)
    return jnp.concatenate([high, middle, low, jnp.zeros((13, row.shape[1]), jnp.bfloat16)], axis=0)


def one_hot_dot(row, chosen, contract):
    parts = lax.dot_general(thirds(row), chosen, (((1,), (contract,)), ((), ())), preferred_element_type=jnp.float32)
    return parts[0:1, :] + (parts[1:2, :] + parts[2:3, :])


def one_hot(index_ref, nodes):
    node = lax.broadcasted_iota(jnp.int32, (nodes, index_ref.shape[1]), 0)
    return jnp.where(node == index_ref[...], 1.0, 0.0).astype(jnp.bfloat16)


def pick_trace(density, send_ref):
    return one_hot_dot(density, one_hot(send_ref, density.shape[1]), 0)


def junction_of(trace, recv_ref, gain_ref, nodes):
    return one_hot_dot(trace * gain_ref[...], one_hot(recv_ref, nodes), 1)


def step_kernel(
    step, order_ref, target_ref, source_ref, lag_ref, place_ref, tgt_ref, src_ref, send_ref, own_ref, *refs
):
    new_refs = refs[:step]
    out_ref, new = refs[step : step + 2]
    work = refs[step + 2 :]
    region, group = place_ref[0], place_ref[2]
    out_ref[...] = jnp.zeros_like(out_ref)
    new[...] = jnp.zeros_like(new)
    for j in range(step):
        new[:, 3 + j] = new_refs[j][...]
    trace = pick_trace(own_ref[...], send_ref)
    tiles = tgt_ref.shape[0] * 2
    for other in range(out_ref.shape[0] // tiles):

        @pl.when(other != region)
        def _():
            out_ref[other * tiles + 2 * group] = jnp.concatenate([trace, trace], axis=0)

    def window_of(member, lag):
        return [new[member, step - lag + i] for i in range(4)]

    def add(tile, rows):
        out_ref[region * tiles + tile] += rows

    lists = (target_ref, source_ref, lag_ref)
    count = order_ref[target_ref.shape[1] + step - 1]
    two_at_a_time(
        count, lambda p: order_ref[p], lists, tgt_ref, src_ref, (work[:4], work[4:]), 1, window_of, add
    )


def first_trace_kernel(send_ref, hist_ref, trace_ref):
    trace = pick_trace(hist_ref[HIST - 1 : HIST, :], send_ref)
    for r in range(trace_ref.shape[0]):
        trace_ref[r] = trace


def density_kernel(step, place_ref, part_ref, recv_ref, gain_ref, inc_ref, self_ref, *refs):
    nodes = inc_ref.shape[1]
    region, partner, group = place_ref[0], place_ref[1], place_ref[2]
    last = step == STEPS - 1
    if step == 0:
        trace_ref, dens_ref, row_ref, past_ref = refs
        groups = part_ref.shape[0] // 2
        fields = []
        for h in range(2):
            total = part_ref[h]
            for g in range(1, groups):
                total = total + part_ref[2 * g + h]
            fields.append(total)
        past = jnp.concatenate(fields, axis=0)
        past_ref[...] = past
        trace = trace_ref[partner]
        rows = [past[8 * h + b : 8 * h + b + 1, :] for h in range(2) for b in range(2)]
    else:
        past_ref = refs[0]
        groups = part_ref.shape[0] // 8
        first = region * (2 * groups)
        rows = []
        for h in range(2):
            total = past_ref[8 * h + 2 * step : 8 * h + 2 * step + 2, :]
            for g in range(groups):
                total = total + part_ref[first + 2 * g + h]
            rows += [total[0:1, :], total[1:2, :]]
        trace = part_ref[(partner * groups + group) * 2][0:1, :]
    field = jnp.concatenate(rows, axis=1)
    junction = junction_of(trace, recv_ref, gain_ref, nodes)
    density = (inc_ref[step : step + 1, :] - field - junction) / self_ref[...]
    if last:
        row_refs, out_ref = refs[1:-1], refs[-1]
        for n in range(STEPS - 1):
            out_ref[n : n + 1, :] = row_refs[n][...]
        out_ref[STEPS - 1 : STEPS, :] = density
    else:
        if step > 0:
            dens_ref, row_ref = refs[1:]
        row_ref[...] = density
        for r in range(nodes // LANES):
            part = density[:, r * LANES : (r + 1) * LANES]
            dens_ref[:, r, :] = jnp.broadcast_to(part, (dens_ref.shape[0], LANES))


def body(
    history,
    incident,
    positions,
    area,
    self_weight,
    pair_target,
    pair_source,
    pair_lag,
    pair_count,
    junc_send,
    junc_recv,
    junc_gain,
    adjacency,
):
    nodes = history.shape[1]
    half = nodes // 2
    jrows = junc_send.shape[1]
    groups, regions, loops = (lax.axis_size(name) for name in ("group", "region", "loop"))
    tiles = 2 * groups
    f32 = jnp.float32
    shape = jax.ShapeDtypeStruct
    region = lax.axis_index("region")
    place = jnp.stack([region, (region + adjacency[0]) % regions, lax.axis_index("group")]).astype(jnp.int32)
    self_row = self_weight.reshape(1, nodes)
    lists = (pair_target, pair_source, pair_lag)
    line_rows = nodes // LANES

    packed = jnp.concatenate([positions, area[None], history[FIRST_STORED:]], axis=0)
    packed = packed.reshape(packed.shape[0], line_rows, LANES)
    packed = jnp.broadcast_to(packed, (loops,) + packed.shape)
    sources = lax.all_to_all(packed, "loop", 0, 0, tiled=True)
    targets = lax.all_to_all(jnp.broadcast_to(positions, (groups, 3, nodes)), "group", 0, 0, tiled=True)
    order = pl.pallas_call(
        order_kernel,
        out_shape=shape((pair_lag.shape[1] + STEPS,), jnp.int32),
        in_specs=[SMEM] * 2,
        out_specs=SMEM,
        compiler_params=SMALL_GRANT,
    )(pair_count, pair_lag)
    trace = pl.pallas_call(
        first_trace_kernel,
        out_shape=shape((regions, 1, jrows), f32),
        in_specs=[VMEM] * 2,
        out_specs=VMEM,
        compiler_params=SMALL_GRANT,
    )(junc_send, history)
    traces = lax.all_to_all(trace, "region", 0, 0, tiled=True)

    def work(steps):
        return [
            pltpu.VMEM((3, half, LANES), f32),
            pltpu.VMEM((3, SUBS, nodes), f32),
            pltpu.VMEM((steps * COEFS, SUBS, nodes), f32),
            pltpu.VMEM((steps, half, LANES), f32),
        ]

    partial_fields = pl.pallas_call(
        history_kernel,
        out_shape=shape((tiles, 2 * STEPS, LANES), f32),
        in_specs=[SMEM] * 4 + [VMEM] * 2,
        out_specs=VMEM,
        scratch_shapes=work(STEPS) * 2,
        compiler_params=PAIR_GRANT,
    )(order, *lists, targets, sources)
    parts = lax.all_to_all(partial_fields, "group", 0, 0, tiled=True)

    dens_shape, row_shape = shape((loops, line_rows, LANES), f32), shape((1, nodes), f32)
    rows, gathered = [], []
    past = None
    for step in range(STEPS):
        if step > 0:
            partial_fields = pl.pallas_call(
                functools.partial(step_kernel, step),
                out_shape=shape((regions * tiles, 2, LANES), f32),
                in_specs=[SMEM] * 5 + [VMEM] * (4 + step),
                out_specs=VMEM,
                scratch_shapes=[pltpu.VMEM((loops, SUBS, line_rows, LANES), f32)] + work(1) * 2,
                compiler_params=PAIR_GRANT,
            )(order, *lists, place, targets, sources, junc_send, rows[-1], *gathered)
            parts = lax.all_to_all(partial_fields, ("region", "group"), 0, 0, tiled=True)
        operands = [place, parts, junc_recv, junc_gain, incident, self_row]
        if step == 0:
            operands += [traces]
            out_shape = [dens_shape, row_shape, shape((2 * 2 * STEPS, LANES), f32)]
        elif step < STEPS - 1:
            operands += [past]
            out_shape = [dens_shape, row_shape]
        else:
            operands += [past] + rows
            out_shape = [shape((STEPS, nodes), f32)]
        results = pl.pallas_call(
            functools.partial(density_kernel, step),
            out_shape=out_shape,
            in_specs=[SMEM] + [VMEM] * (len(operands) - 1),
            out_specs=[VMEM] * len(out_shape),
            compiler_params=SMALL_GRANT,
        )(*operands)
        if step == 0:
            past = results[2]
        if step < STEPS - 1:
            rows.append(results[1])
            gathered.append(lax.all_to_all(results[0], "loop", 0, 0, tiled=True))
    return results[0]


def solution(mesh):
    blocks = ("region", "group", "loop")
    in_specs = (
        P(None, blocks),
        P(None, blocks),
        P(None, blocks),
        P(blocks),
        P(blocks),
        P(blocks, None),
        P(blocks, None),
        P(blocks, None),
        P(blocks),
        P(blocks, None),
        P(blocks, None),
        P(blocks, None),
        P(blocks),
    )
    return jax.shard_map(body, mesh=mesh, in_specs=in_specs, out_specs=P(None, blocks), check_vma=False)
```

profile of v0, /device:TPU:2, one launch (start us, length us, event | category | flops | bytes accessed | tf_op | source)
XLA Modules:
  0.0 177.1 jit_solution(15026425755424777477)
XLA Ops:
  0.0 1.4 broadcast_in_dim.7
  1.4 0.0 copy-start.9
  1.4 0.0 copy-start.1
  1.4 15.8 %all-to-all-start = ((f32[16,3,512]{2,1,0:T(4,128)}), f32[16,3,512]{2,1,0:T(4,128)S(1)}, u32[]{:S(2)}, u32[]{:S(2)}) async-start(f32[16,3,512]{2,1,0:T(4,128)} %broadcast_in_dim.7), calls=%async_computation | async-start | bytes 262144 | tf_op jit(solution)/shard_map/all_to_all | solution.py:288
  17.2 0.0 copy-done.9
  17.2 0.0 copy-done.1
  17.2 0.0 copy-start.10
  17.2 0.7 copy-done.10
  17.9 11.8 %all-to-all-done.tgt_ref = f32[16,3,512]{2,1,0:T(4,128)S(1)} async-done(((f32[16,3,512]{2,1,0:T(4,128)}), f32[16,3,512]{2,1,0:T(4,128)S(1)}, u32[]{:S(2)}, u32[]{:S(2)}) %all-to-all-start) | async-done | bytes 98336 | tf_op jit(solution)/shard_map/all_to_all | solution.py:288
  29.7 0.8 broadcast_in_dim.8
  30.5 0.0 copy-start.6
  30.5 5.0 %all-to-all-start.1 = ((f32[8,19,4,128]{3,2,1,0:T(4,128)}), f32[8,19,4,128]{3,2,1,0:T(4,128)S(1)}, u32[]{:S(2)}, u32[]{:S(2)}) async-start(f32[8,19,4,128]{3,2,1,0:T(4,128)} %broadcast_in_dim.8), calls=%async_computation.1 | async-start | bytes 622592 | tf_op jit(solution)/shard_map/all_to_all | solution.py:287
  35.4 0.0 copy-done.6
  35.4 0.7 shard_map.129
  36.2 5.8 %all-to-all-done.1.src_ref = f32[8,19,4,128]{3,2,1,0:T(4,128)S(1)} async-done(((f32[8,19,4,128]{3,2,1,0:T(4,128)}), f32[8,19,4,128]{3,2,1,0:T(4,128)S(1)}, u32[]{:S(2)}, u32[]{:S(2)}) %all-to-all-start.1) | async-done | bytes 311328 | tf_op jit(solution)/shard_map/all_to_all | solution.py:287
  42.0 4.5 %all-to-all-start.3 = ((f32[4,1,128]{2,1,0:T(1,128)}), f32[4,1,128]{2,1,0:T(1,128)S(1)}, u32[]{:S(2)}, u32[]{:S(2)}) async-start(f32[4,1,128]{2,1,0:T(1,128)} %shard_map.129), calls=%async_computation.3 | async-start | bytes 4096 | tf_op jit(solution)/shard_map/all_to_all | solution.py:303
  46.5 0.0 copy-start.3
  47.2 0.0 copy-done.3
  47.2 0.0 copy-start.4
  47.2 0.0 copy-start.5
  47.2 1.3 shard_map.127.order_ref
  48.5 0.0 copy-done.4
  48.5 0.0 copy-done.5
  48.5 19.7 %shard_map.128 = f32[32,8,128]{2,1,0:T(8,128)} custom-call(s32[28]{0:T(128)S(1)} %shard_map.127.order_ref, s32[1,24]{1,0:T(1,128)S(1)} %copy-done.4, s32[1,24]{1,0:T(1,128)S(1)} %copy-done.5, s32[1,24]{1,0:T(1,128)S(1)} %copy-done.3, f32[16,3,512]{2,1,0:T(4,128)S(1)} %all-to-all-done.tgt_ref, f32[8,19,4,128]{3,2,1,0:T(4,128)S(1)} %all-to-all-done.1.src_ref), custom_call_target="tpu_custom_call" | custom-call | tf_op jit(solution)/shard_map/pallas_call | solution.py:313
  68.2 0.0 all-to-all-done.3.refs_0_
  68.2 4.8 %all-to-all-start.2 = ((f32[32,8,128]{2,1,0:T(8,128)}), f32[32,8,128]{2,1,0:T(8,128)S(1)}, u32[]{:S(2)}, u32[]{:S(2)}) async-start(f32[32,8,128]{2,1,0:T(8,128)} %shard_map.128), calls=%async_computation.2 | async-start | bytes 262144 | tf_op jit(solution)/shard_map/all_to_all | solution.py:321
  73.7 0.0 copy-start
  73.7 0.0 copy-start.2
  73.7 0.1 pad_add_fusion.place_ref
  73.8 0.0 copy-start.7
  73.8 0.0 copy-start.8
  73.8 11.7 %all-to-all-done.2.part_ref = f32[32,8,128]{2,1,0:T(8,128)S(1)} async-done(((f32[32,8,128]{2,1,0:T(8,128)}), f32[32,8,128]{2,1,0:T(8,128)S(1)}, u32[]{:S(2)}, u32[]{:S(2)}) %all-to-all-start.2) | async-done | bytes 131104 | tf_op jit(solution)/shard_map/all_to_all | solution.py:321
  85.5 0.0 copy-done
  85.5 0.0 copy-done.2
  85.5 0.0 copy-done.7
  85.6 0.0 copy-done.8
  85.6 0.7 shard_map.130
  86.3 8.0 %all_to_all.50.refs_0_ = f32[8,4,128]{2,1,0:T(4,128)S(1)} all-to-all(f32[8,4,128]{2,1,0:T(4,128)S(1)} %get-tuple-element.13), channel_id=1, replica_groups=mesh['region'=4,'group'=16,'loop'=8] {'loop'}, dimensions={0} | all-to-all | bytes 32768 | tf_op jit(solution)/shard_map/all_to_all | solution.py:358
  94.3 1.6 shard_map.131
  96.0 20.3 %all_to_all.51.part_ref = f32[128,2,128]{2,1,0:T(2,128)S(1)} all-to-all(f32[128,2,128]{2,1,0:T(2,128)S(1)} %shard_map.131), channel_id=1, replica_groups=mesh['region'=4,'group'=16,'loop'=8] {'region','group'}, dimensions={0} | all-to-all | bytes 262144 | tf_op jit(solution)/shard_map/all_to_all | solution.py:336
  116.2 0.7 shard_map.132
  117.0 8.0 %all_to_all.52.refs_1_ = f32[8,4,128]{2,1,0:T(4,128)S(1)} all-to-all(f32[8,4,128]{2,1,0:T(4,128)S(1)} %get-tuple-element.16), channel_id=1, replica_groups=mesh['region'=4,'group'=16,'loop'=8] {'loop'}, dimensions={0} | all-to-all | bytes 32768 | tf_op jit(solution)/shard_map/all_to_all | solution.py:358
  124.9 2.5 %shard_map.133 = f32[128,2,128]{2,1,0:T(2,128)S(1)} custom-call(s32[28]{0:T(128)S(1)} %shard_map.127.order_ref, s32[1,24]{1,0:T(1,128)S(1)} %copy-done.4, s32[1,24]{1,0:T(1,128)S(1)} %copy-done.5, s32[1,24]{1,0:T(1,128)S(1)} %copy-done.3, s32[3]{0:T(128)S(1)} %pad_add_fusion.place_ref, f32[16,3,512]{2,1,0:T(4,128)S(1)} %all-to-all-done.tgt_ref, ...), custom_call_target="tpu_custom_call" | custom-call | tf_op jit(solution)/shard_map/pallas_call | solution.py:328
  127.4 17.9 %all_to_all.53.part_ref = f32[128,2,128]{2,1,0:T(2,128)S(1)} all-to-all(f32[128,2,128]{2,1,0:T(2,128)S(1)} %shard_map.133), channel_id=1, replica_groups=mesh['region'=4,'group'=16,'loop'=8] {'region','group'}, dimensions={0} | all-to-all | bytes 262144 | tf_op jit(solution)/shard_map/all_to_all | solution.py:336
  145.4 0.7 shard_map.134
  146.1 7.7 %all_to_all.54.refs_2_ = f32[8,4,128]{2,1,0:T(4,128)S(1)} all-to-all(f32[8,4,128]{2,1,0:T(4,128)S(1)} %get-tuple-element.18), channel_id=1, replica_groups=mesh['region'=4,'group'=16,'loop'=8] {'loop'}, dimensions={0} | all-to-all | bytes 32768 | tf_op jit(solution)/shard_map/all_to_all | solution.py:358
  153.8 3.4 %shard_map.135 = f32[128,2,128]{2,1,0:T(2,128)S(1)} custom-call(s32[28]{0:T(128)S(1)} %shard_map.127.order_ref, s32[1,24]{1,0:T(1,128)S(1)} %copy-done.4, s32[1,24]{1,0:T(1,128)S(1)} %copy-done.5, s32[1,24]{1,0:T(1,128)S(1)} %copy-done.3, s32[3]{0:T(128)S(1)} %pad_add_fusion.place_ref, f32[16,3,512]{2,1,0:T(4,128)S(1)} %all-to-all-done.tgt_ref, ...), custom_call_target="tpu_custom_call" | custom-call | tf_op jit(solution)/shard_map/pallas_call | solution.py:328
  157.2 18.6 %all_to_all.55.part_ref = f32[128,2,128]{2,1,0:T(2,128)S(1)} all-to-all(f32[128,2,128]{2,1,0:T(2,128)S(1)} %shard_map.135), channel_id=1, replica_groups=mesh['region'=4,'group'=16,'loop'=8] {'region','group'}, dimensions={0} | all-to-all | bytes 262144 | tf_op jit(solution)/shard_map/all_to_all | solution.py:336
  175.8 1.3 shard_map.136
  (4 shorter events, 0.0 us)
Async XLA Ops:
  1.4 15.8 %copy-start.9 = (f32[3,512]{1,0:T(4,128)S(1)}, f32[3,512]{1,0:T(4,128)}, u32[]{:S(2)}) copy-start(f32[3,512]{1,0:T(4,128)} %param.15) | copy-start | bytes 18436
  1.4 15.8 %copy-start.1 = (f32[16,512]{1,0:T(8,128)S(1)}, f32[16,512]{1,0:T(8,128)}, u32[]{:S(2)}) copy-start(f32[16,512]{1,0:T(8,128)} %hist_ref.1) | copy-start | bytes 98308
  1.4 28.3 %all-to-all-start = ((f32[16,3,512]{2,1,0:T(4,128)}), f32[16,3,512]{2,1,0:T(4,128)S(1)}, u32[]{:S(2)}, u32[]{:S(2)}) async-start(f32[16,3,512]{2,1,0:T(4,128)} %broadcast_in_dim.7), calls=%async_computation | async-start | bytes 262144 | tf_op jit(solution)/shard_map/all_to_all | solution.py:288
  17.2 0.7 copy-start.10
  30.5 5.0 %copy-start.6 = (s32[1,128]{1,0:T(1,128)S(1)}, s32[1,128]{1,0:T(1,128)}, u32[]{:S(2)}) copy-start(s32[1,128]{1,0:T(1,128)} %send_ref.7) | copy-start | bytes 1540
  30.5 11.5 %all-to-all-start.1 = ((f32[8,19,4,128]{3,2,1,0:T(4,128)}), f32[8,19,4,128]{3,2,1,0:T(4,128)S(1)}, u32[]{:S(2)}, u32[]{:S(2)}) async-start(f32[8,19,4,128]{3,2,1,0:T(4,128)} %broadcast_in_dim.8), calls=%async_computation.1 | async-start | bytes 622592 | tf_op jit(solution)/shard_map/all_to_all | solution.py:287
  42.0 26.2 %all-to-all-start.3 = ((f32[4,1,128]{2,1,0:T(1,128)}), f32[4,1,128]{2,1,0:T(1,128)S(1)}, u32[]{:S(2)}, u32[]{:S(2)}) async-start(f32[4,1,128]{2,1,0:T(1,128)} %shard_map.129), calls=%async_computation.3 | async-start | bytes 4096 | tf_op jit(solution)/shard_map/all_to_all | solution.py:303
  46.5 0.7 copy-start.3
  47.2 1.3 copy-start.4
  47.2 1.3 copy-start.5
  68.2 17.3 %all-to-all-start.2 = ((f32[32,8,128]{2,1,0:T(8,128)}), f32[32,8,128]{2,1,0:T(8,128)S(1)}, u32[]{:S(2)}, u32[]{:S(2)}) async-start(f32[32,8,128]{2,1,0:T(8,128)} %shard_map.128), calls=%async_computation.2 | async-start | bytes 262144 | tf_op jit(solution)/shard_map/all_to_all | solution.py:321
  73.7 11.8 %copy-start = (f32[4,512]{1,0:T(4,128)S(1)}, f32[4,512]{1,0:T(4,128)}, u32[]{:S(2)}) copy-start(f32[4,512]{1,0:T(4,128)} %inc_ref.7) | copy-start | bytes 24580
  73.7 11.8 %copy-start.2 = (f32[512]{0:T(512)S(1)}, f32[512]{0:T(512)}, u32[]{:S(2)}) copy-start(f32[512]{0:T(512)} %param.17) | copy-start | bytes 6148
  73.8 11.7 %copy-start.7 = (s32[1,128]{1,0:T(1,128)S(1)}, s32[1,128]{1,0:T(1,128)}, u32[]{:S(2)}) copy-start(s32[1,128]{1,0:T(1,128)} %recv_ref.7) | copy-start | bytes 1540
  73.8 11.7 %copy-start.8 = (f32[1,128]{1,0:T(1,128)S(1)}, f32[1,128]{1,0:T(1,128)}, u32[]{:S(2)}) copy-start(f32[1,128]{1,0:T(1,128)} %gain_ref.7) | copy-start | bytes 1540
where the time goes:
time: 178 us; the launch traced here: 177 us
  blocking collectives  80.6 us (45%)
  Pallas kernels  32.6 us (18%)
  starting transfers between devices  30.1 us (17%)
  waiting for transfers between devices  29.3 us (16%)
  local copies, waits for them, and re-layouts  2.87 us (2%)
    all_to_all x3, blocking collectives, body(): lax.all_to_all(partial_fields, ('region', 'group'), 0, 0, tiled=True)  56.9 us
    all_to_all x3, blocking collectives, body(): gathered.append(lax.all_to_all(results[0], 'loop', 0, 0, tiled=True))  23.7 us
    pallas_call x1, Pallas kernels, body(): pl.pallas_call(history_kernel, out_shape=shape((tiles, 2 * STEPS, LANES),...  19.7 us
    all_to_all x1, starting transfers between devices, body(): lax.all_to_all(jnp.broadcast_to(positions, (groups, 3, nodes)), 'group',...  15.8 us
    all_to_all x1, waiting for transfers between devices, body(): lax.all_to_all(jnp.broadcast_to(positions, (groups, 3, nodes)), 'group',...  11.8 us
    all_to_all x1, waiting for transfers between devices, body(): parts = lax.all_to_all(partial_fields, 'group', 0, 0, tiled=True)  11.7 us
    pallas_call x3, Pallas kernels, body(): pl.pallas_call(functools.partial(step_kernel, step), out_shape=shape((reg...  7.49 us
    all_to_all x1, waiting for transfers between devices, body(): sources = lax.all_to_all(packed, 'loop', 0, 0, tiled=True)  5.83 us
  transfers between devices with their start and end apart: 4, of which 3 were waited for; matrix products, arithmetic and copies ran while one was open for 0% of the time, Pallas kernels for 12%

commit v1 on v0

--- a/solution.py
+++ b/solution.py
@@ -17,9 +17,12 @@
 STORED_ROW = 4
 FIRST_STORED = 1
 COEFS = 4
+NEAR = 12
+NEAR_COEFS = STEPS - 1
 
 
 PAIR_GRANT = pltpu.CompilerParams(vmem_limit_bytes=12 * 2**20)
+NEAR_GRANT = pltpu.CompilerParams(vmem_limit_bytes=12 * 2**20)
 SMALL_GRANT = pltpu.CompilerParams(vmem_limit_bytes=4 * 2**20)
 VMEM = pl.BlockSpec(memory_space=pltpu.VMEM)
 SMEM = pl.BlockSpec(memory_space=pltpu.SMEM)
@@ -144,6 +147,59 @@
     )
 
 
+def near_kernel(order_ref, target_ref, source_ref, tgt_ref, src_ref, near_ref, *work):
+    lines = src_ref.shape[2]
+    count = jnp.minimum(order_ref[target_ref.shape[1] + STEPS - 2], NEAR)
+    spaces = (work[:2], work[2:])
+
+    def turn_fn(turn, carry):
+        for side, (tb, geo) in enumerate(spaces):
+            slot = jnp.minimum(2 * turn + side, count - 1)
+            p = order_ref[slot]
+            tile, member = target_ref[0, p], source_ref[0, p]
+            spread_targets(tgt_ref, tile, tb)
+            for k in range(3):
+                spread(geo, k, src_ref[member, k])
+            spread(geo, 3, src_ref[member, AREA_ROW] * (1.0 / 6.0))
+
+            def block_fn(i, carry):
+                rows = pl.ds(pl.multiple_of(i * SUBS, SUBS), SUBS)
+                coords = [tb[k, rows, :] for k in range(3)]
+                for c in range(lines):
+                    cols = slice(c * LANES, (c + 1) * LANES)
+                    dist_sq = None
+                    for k in range(3):
+                        delta = coords[k] - geo[k, :, cols]
+                        square = delta * delta
+                        dist_sq = square if dist_sq is None else dist_sq + square
+                    weight = geo[3, :, cols] * lax.rsqrt(dist_sq + SOFTEN)
+                    u = 1.0 / (1.0 + dist_sq)
+                    square = u * u
+                    cube = square * u
+                    near_ref[slot, 0, c, rows, :] = weight * cube
+                    near_ref[slot, 1, c, rows, :] = weight * (1.0 + 3.0 * (u + square - cube))
+                    near_ref[slot, 2, c, rows, :] = weight * (4.0 + 3.0 * (cube - 2.0 * square))
+                return carry
+
+            lax.fori_loop(0, tb.shape[1] // SUBS, block_fn, 0, unroll=tb.shape[1] // SUBS)
+        return carry
+
+    lax.fori_loop(0, (count + 1) // 2, turn_fn, 0)
+
+
+def near_sums(step, near_ref, slot, new_ref, member, lag):
+    total = None
+    for k in range(step):
+        density = new_ref[member, 3 + step - lag - k]
+        for c in range(density.shape[0]):
+            term = near_ref[slot, k, c] * density[c : c + 1, :]
+            total = term if total is None else total + term
+    halves = [
+        jnp.sum(jnp.transpose(total[b * LANES : (b + 1) * LANES], (1, 0)), axis=0, keepdims=True) for b in range(2)
+    ]
+    return jnp.concatenate(halves, axis=0)
+
+
 def thirds(row):
     high = row.astype(jnp.bfloat16)
     rest = row - high.astype(jnp.float32)
@@ -171,7 +227,7 @@
 
 
 def step_kernel(
-    step, order_ref, target_ref, source_ref, lag_ref, place_ref, tgt_ref, src_ref, send_ref, own_ref, *refs
+    step, order_ref, target_ref, source_ref, lag_ref, place_ref, near_ref, tgt_ref, src_ref, send_ref, own_ref, *refs
 ):
     new_refs = refs[:step]
     out_ref, new = refs[step : step + 2]
@@ -195,10 +251,25 @@
     def add(tile, rows):
         out_ref[region * tiles + tile] += rows
 
+    count = order_ref[target_ref.shape[1] + step - 1]
+    kept = jnp.minimum(count, NEAR)
+
+    def turn_fn(turn, carry):
+        sums = []
+        for side in range(2):
+            place = 2 * turn + side
+            slot = jnp.minimum(place, kept - 1)
+            p = order_ref[slot]
+            share = near_sums(step, near_ref, slot, new, source_ref[0, p], lag_ref[0, p])
+            sums.append((target_ref[0, p], jnp.where(place < kept, share, 0.0)))
+        for tile, share in sums:
+            add(tile, share)
+        return carry
+
+    lax.fori_loop(0, (kept + 1) // 2, turn_fn, 0)
     lists = (target_ref, source_ref, lag_ref)
-    count = order_ref[target_ref.shape[1] + step - 1]
     two_at_a_time(
-        count, lambda p: order_ref[p], lists, tgt_ref, src_ref, (work[:4], work[4:]), 1, window_of, add
+        count - kept, lambda p: order_ref[NEAR + p], lists, tgt_ref, src_ref, (work[:4], work[4:]), 1, window_of, add
     )
 
 
@@ -318,6 +389,16 @@
         scratch_shapes=work(STEPS) * 2,
         compiler_params=PAIR_GRANT,
     )(order, *lists, targets, sources)
+    order, place, partial_fields, traces = lax.optimization_barrier((order, place, partial_fields, traces))
+    near = pl.pallas_call(
+        near_kernel,
+        out_shape=shape((NEAR, NEAR_COEFS, line_rows, half, LANES), f32),
+        in_specs=[SMEM] * 3 + [VMEM] * 2,
+        out_specs=VMEM,
+        scratch_shapes=[pltpu.VMEM((3, half, LANES), f32), pltpu.VMEM((4, SUBS, nodes), f32)] * 2,
+        compiler_params=NEAR_GRANT,
+    )(order, pair_target, pair_source, targets, sources)
+    near, partial_fields = lax.optimization_barrier((near, partial_fields))
     parts = lax.all_to_all(partial_fields, "group", 0, 0, tiled=True)
 
     dens_shape, row_shape = shape((loops, line_rows, LANES), f32), shape((1, nodes), f32)
@@ -328,11 +409,11 @@
             partial_fields = pl.pallas_call(
                 functools.partial(step_kernel, step),
                 out_shape=shape((regions * tiles, 2, LANES), f32),
-                in_specs=[SMEM] * 5 + [VMEM] * (4 + step),
+                in_specs=[SMEM] * 5 + [VMEM] * (5 + step),
                 out_specs=VMEM,
                 scratch_shapes=[pltpu.VMEM((loops, SUBS, line_rows, LANES), f32)] + work(1) * 2,
-                compiler_params=PAIR_GRANT,
-            )(order, *lists, place, targets, sources, junc_send, rows[-1], *gathered)
+                compiler_params=NEAR_GRANT,
+            )(order, *lists, place, near, targets, sources, junc_send, rows[-1], *gathered)
             parts = lax.all_to_all(partial_fields, ("region", "group"), 0, 0, tiled=True)
         operands = [place, parts, junc_recv, junc_gain, incident, self_row]
         if step == 0:

time: 178 us -> 179 us (level)
  waiting for transfers between devices: 29.3 us -> 14.1 us
  blocking collectives: 80.6 us -> 95.6 us
  local copies, waits for them, and re-layouts: 2.87 us -> 9.02 us
  starting transfers between devices: 30.1 us -> 25 us
    all_to_all x0 -> x1, blocking collectives: none -> 16.9 us  [body(): parts = lax.all_to_all(partial_fields, 'group', 0, 0, tiled=True)]
    all_to_all x1 -> x0, waiting for transfers between devices: 11.7 us -> none  [body(): parts = lax.all_to_all(partial_fields, 'group', 0, 0, tiled=True)]
    all_to_all x1 -> x0, starting transfers between devices: 4.84 us -> none  [body(): parts = lax.all_to_all(partial_fields, 'group', 0, 0, tiled=True)]
    unnamed x22 -> x32, local copies, waits for them, and re-layouts: 0.7 us -> 5.36 us
    all_to_all x3, blocking collectives: 56.9 us -> 52.7 us  [body(): lax.all_to_all(partial_fields, ('region', 'group'), 0, 0, tiled=True)]
    pallas_call x3, Pallas kernels: 7.49 us -> 3.88 us  [body(): pl.pallas_call(functools.partial(step_kernel, step), out_shape=shape((reg...]
    pallas_call x0 -> x1, Pallas kernels: none -> 3.57 us  [body(): pl.pallas_call(near_kernel, out_shape=shape((NEAR, NEAR_COEFS, line_rows,...]
    all_to_all x3, blocking collectives: 23.7 us -> 26 us  [body(): gathered.append(lax.all_to_all(results[0], 'loop', 0, 0, tiled=True))]
  transfers between devices with their start and end apart: 4 -> 3, of which waited for: 3 -> 2; matrix products, arithmetic and copies ran while one was open for 0% -> 1% of each run, Pallas kernels for 12% -> 12%
where the time goes in v1:
time: 179 us; the launch traced here: 178 us
  blocking collectives  95.6 us (53%)
  Pallas kernels  31.9 us (18%)
  starting transfers between devices  25 us (14%)
  waiting for transfers between devices  14.1 us (8%)
  local copies, waits for them, and re-layouts  9.02 us (5%)
    all_to_all x3, blocking collectives, body(): lax.all_to_all(partial_fields, ('region', 'group'), 0, 0, tiled=True)  52.7 us
    all_to_all x3, blocking collectives, body(): gathered.append(lax.all_to_all(results[0], 'loop', 0, 0, tiled=True))  26 us
    pallas_call x1, Pallas kernels, body(): pl.pallas_call(history_kernel, out_shape=shape((tiles, 2 * STEPS, LANES),...  19 us
    all_to_all x1, blocking collectives, body(): parts = lax.all_to_all(partial_fields, 'group', 0, 0, tiled=True)  16.9 us
    all_to_all x1, starting transfers between devices, body(): lax.all_to_all(jnp.broadcast_to(positions, (groups, 3, nodes)), 'group',...  15.6 us
    all_to_all x1, waiting for transfers between devices, body(): lax.all_to_all(jnp.broadcast_to(positions, (groups, 3, nodes)), 'group',...  10.3 us
    unnamed x32, local copies, waits for them, and re-layouts  5.36 us
    all_to_all x1, starting transfers between devices, body(): sources = lax.all_to_all(packed, 'loop', 0, 0, tiled=True)  4.83 us
  transfers between devices with their start and end apart: 3, of which 2 were waited for; matrix products, arithmetic and copies ran while one was open for 1% of the time, Pallas kernels for 12%

profile of v1, /device:TPU:2, one launch (start us, length us, event | category | flops | bytes accessed | tf_op | source)
XLA Modules:
  0.0 177.9 jit_solution(14618078294894201298)
XLA Ops:
  0.0 0.0 copy-start.13
  0.0 0.0 copy-start.11
  0.0 0.0 copy-start.8
  0.0 0.0 copy-start.5
  0.0 0.0 copy-start.15
  0.0 0.0 copy-start.14
  0.0 0.0 copy-start
  0.1 0.0 copy-start.2
  0.1 1.4 broadcast_in_dim.7
  1.5 15.6 %all-to-all-start = ((f32[16,3,512]{2,1,0:T(4,128)}), f32[16,3,512]{2,1,0:T(4,128)S(1)}, u32[]{:S(2)}, u32[]{:S(2)}) async-start(f32[16,3,512]{2,1,0:T(4,128)} %broadcast_in_dim.7), calls=%async_computation | async-start | bytes 262144 | tf_op jit(solution)/shard_map/all_to_all | solution.py:359
  17.1 0.7 concatenate.10
  17.9 0.8 slice.3
  18.6 0.7 pad_maximum_fusion
  19.3 10.3 %all-to-all-done.tgt_ref = f32[16,3,512]{2,1,0:T(4,128)S(1)} async-done(((f32[16,3,512]{2,1,0:T(4,128)}), f32[16,3,512]{2,1,0:T(4,128)S(1)}, u32[]{:S(2)}, u32[]{:S(2)}) %all-to-all-start) | async-done | bytes 98336 | tf_op jit(solution)/shard_map/all_to_all | solution.py:359
  29.7 0.8 broadcast_in_dim.8
  30.4 4.8 %all-to-all-start.1 = ((f32[8,19,4,128]{3,2,1,0:T(4,128)}), f32[8,19,4,128]{3,2,1,0:T(4,128)S(1)}, u32[]{:S(2)}, u32[]{:S(2)}) async-start(f32[8,19,4,128]{3,2,1,0:T(4,128)} %broadcast_in_dim.8), calls=%async_computation.1 | async-start | bytes 622592 | tf_op jit(solution)/shard_map/all_to_all | solution.py:358
  35.9 0.0 copy-start.1
  35.9 0.7 copy-done.1
  36.7 0.0 copy-start.12
  36.7 0.7 copy-done.12
  37.3 0.7 shard_map.129
  38.1 3.8 %all-to-all-done.1.src_ref = f32[8,19,4,128]{3,2,1,0:T(4,128)S(1)} async-done(((f32[8,19,4,128]{3,2,1,0:T(4,128)}), f32[8,19,4,128]{3,2,1,0:T(4,128)S(1)}, u32[]{:S(2)}, u32[]{:S(2)}) %all-to-all-start.1) | async-done | bytes 311328 | tf_op jit(solution)/shard_map/all_to_all | solution.py:358
  41.8 4.5 %all-to-all-start.2 = ((f32[4,1,128]{2,1,0:T(1,128)}), f32[4,1,128]{2,1,0:T(1,128)S(1)}, u32[]{:S(2)}, u32[]{:S(2)}) async-start(f32[4,1,128]{2,1,0:T(1,128)} %shard_map.129), calls=%async_computation.2 | async-start | bytes 4096 | tf_op jit(solution)/shard_map/all_to_all | solution.py:374
  46.3 0.1 pad_add_fusion.place_ref
  47.1 0.0 copy-start.9
  47.1 0.6 copy-done.9
  47.7 1.3 shard_map.127.order_ref
  49.0 0.0 copy-start.3
  49.1 0.6 copy-done.3
  49.7 0.0 copy-start.6
  49.7 0.7 copy-done.6
  50.4 0.0 copy-start.10
  50.4 0.7 copy-done.10
  51.0 19.0 %shard_map.128 = f32[32,8,128]{2,1,0:T(8,128)S(1)} custom-call(s32[28]{0:T(128)S(1)} %shard_map.127.order_ref, s32[1,24]{1,0:T(1,128)S(1)} %copy-done.3, s32[1,24]{1,0:T(1,128)S(1)} %copy-done.6, s32[1,24]{1,0:T(1,128)S(1)} %copy-done.10, f32[16,3,512]{2,1,0:T(4,128)S(1)} %all-to-all-done.tgt_ref, f32[8,19,4,128]{3,2,1,0:T(4,128)S(1)} %all-to-all-done.1.src_ref), custom_call_target="tpu_custom_call" | custom-call | tf_op jit(solution)/shard_map/pallas_call | solution.py:384
  70.0 0.0 all-to-all-done.2.refs_0_
  70.0 0.0 copy-start.4
  70.0 0.6 copy-done.4
  70.7 0.0 copy-start.7
  70.7 0.7 copy-done.7
  71.3 3.6 %shard_map.130.near_ref = f32[12,3,4,256,128]{4,3,2,1,0:T(8,128)S(1)} custom-call(s32[28]{0:T(128)S(1)} %shard_map.127.order_ref, s32[1,24]{1,0:T(1,128)S(1)} %copy-done.4, s32[1,24]{1,0:T(1,128)S(1)} %copy-done.7, f32[16,3,512]{2,1,0:T(4,128)S(1)} %all-to-all-done.tgt_ref, f32[8,19,4,128]{3,2,1,0:T(4,128)S(1)} %all-to-all-done.1.src_ref), custom_call_target="tpu_custom_call" | custom-call | tf_op jit(solution)/shard_map/pallas_call | solution.py:393
  74.9 16.9 %all_to_all.50.part_ref = f32[32,8,128]{2,1,0:T(8,128)S(1)} all-to-all(f32[32,8,128]{2,1,0:T(8,128)S(1)} %shard_map.128), channel_id=1, replica_groups=mesh['region'=4,'group'=16,'loop'=8] {'group'}, dimensions={0} | all-to-all | bytes 262144 | tf_op jit(solution)/shard_map/all_to_all | solution.py:402
  91.9 0.0 copy-done.15
  91.9 0.0 copy-done.14
  91.9 0.0 copy-done
  91.9 0.0 copy-done.2
  91.9 0.7 shard_map.131
  92.6 10.6 %all_to_all.51.refs_0_ = f32[8,4,128]{2,1,0:T(4,128)S(1)} all-to-all(f32[8,4,128]{2,1,0:T(4,128)S(1)} %get-tuple-element.25), channel_id=1, replica_groups=mesh['region'=4,'group'=16,'loop'=8] {'loop'}, dimensions={0} | all-to-all | bytes 32768 | tf_op jit(solution)/shard_map/all_to_all | solution.py:439
  103.3 0.0 copy-done.13
  103.3 0.0 copy-done.11
  103.3 0.0 copy-done.8
  103.3 0.0 copy-done.5
  103.3 0.9 shard_map.132
  104.2 19.2 %all_to_all.52.part_ref = f32[128,2,128]{2,1,0:T(2,128)S(1)} all-to-all(f32[128,2,128]{2,1,0:T(2,128)S(1)} %shard_map.132), channel_id=1, replica_groups=mesh['region'=4,'group'=16,'loop'=8] {'region','group'}, dimensions={0} | all-to-all | bytes 262144 | tf_op jit(solution)/shard_map/all_to_all | solution.py:417
  123.5 0.7 shard_map.133
  124.2 7.6 %all_to_all.53.refs_1_ = f32[8,4,128]{2,1,0:T(4,128)S(1)} all-to-all(f32[8,4,128]{2,1,0:T(4,128)S(1)} %get-tuple-element.28), channel_id=1, replica_groups=mesh['region'=4,'group'=16,'loop'=8] {'loop'}, dimensions={0} | all-to-all | bytes 32768 | tf_op jit(solution)/shard_map/all_to_all | solution.py:439
  131.8 1.2 shard_map.134
  133.1 16.5 %all_to_all.54.part_ref = f32[128,2,128]{2,1,0:T(2,128)S(1)} all-to-all(f32[128,2,128]{2,1,0:T(2,128)S(1)} %shard_map.134), channel_id=1, replica_groups=mesh['region'=4,'group'=16,'loop'=8] {'region','group'}, dimensions={0} | all-to-all | bytes 262144 | tf_op jit(solution)/shard_map/all_to_all | solution.py:417
  149.5 0.7 shard_map.135
  150.3 7.7 %all_to_all.55.refs_2_ = f32[8,4,128]{2,1,0:T(4,128)S(1)} all-to-all(f32[8,4,128]{2,1,0:T(4,128)S(1)} %get-tuple-element.30), channel_id=1, replica_groups=mesh['region'=4,'group'=16,'loop'=8] {'loop'}, dimensions={0} | all-to-all | bytes 32768 | tf_op jit(solution)/shard_map/all_to_all | solution.py:439
  157.9 1.7 shard_map.136
  159.6 17.0 %all_to_all.56.part_ref = f32[128,2,128]{2,1,0:T(2,128)S(1)} all-to-all(f32[128,2,128]{2,1,0:T(2,128)S(1)} %shard_map.136), channel_id=1, replica_groups=mesh['region'=4,'group'=16,'loop'=8] {'region','group'}, dimensions={0} | all-to-all | bytes 262144 | tf_op jit(solution)/shard_map/all_to_all | solution.py:417
  176.6 1.3 shard_map.137
  (1 shorter events, 0.0 us)
Async XLA Ops:
  0.0 103.3 %copy-start.13 = (s32[1,128]{1,0:T(1,128)S(1)}, s32[1,128]{1,0:T(1,128)}, u32[]{:S(2)}) copy-start(s32[1,128]{1,0:T(1,128)} %send_ref.7) | copy-start | bytes 1540
  0.0 103.3 %copy-start.11 = (s32[1,24]{1,0:T(1,128)S(1)}, s32[1,24]{1,0:T(1,128)}, u32[]{:S(2)}) copy-start(s32[1,24]{1,0:T(1,128)} %lag_ref.9) | copy-start | bytes 292
  0.0 103.3 %copy-start.8 = (s32[1,24]{1,0:T(1,128)S(1)}, s32[1,24]{1,0:T(1,128)}, u32[]{:S(2)}) copy-start(s32[1,24]{1,0:T(1,128)} %source_ref.9) | copy-start | bytes 292
  0.0 103.3 %copy-start.5 = (s32[1,24]{1,0:T(1,128)S(1)}, s32[1,24]{1,0:T(1,128)}, u32[]{:S(2)}) copy-start(s32[1,24]{1,0:T(1,128)} %target_ref.9) | copy-start | bytes 292
  0.0 91.8 %copy-start.15 = (f32[1,128]{1,0:T(1,128)S(1)}, f32[1,128]{1,0:T(1,128)}, u32[]{:S(2)}) copy-start(f32[1,128]{1,0:T(1,128)} %gain_ref.7) | copy-start | bytes 1540
  0.0 91.8 %copy-start.14 = (s32[1,128]{1,0:T(1,128)S(1)}, s32[1,128]{1,0:T(1,128)}, u32[]{:S(2)}) copy-start(s32[1,128]{1,0:T(1,128)} %recv_ref.7) | copy-start | bytes 1540
  0.0 91.8 %copy-start = (f32[4,512]{1,0:T(4,128)S(1)}, f32[4,512]{1,0:T(4,128)}, u32[]{:S(2)}) copy-start(f32[4,512]{1,0:T(4,128)} %inc_ref.7) | copy-start | bytes 24580
  0.1 91.8 %copy-start.2 = (f32[512]{0:T(512)S(1)}, f32[512]{0:T(512)}, u32[]{:S(2)}) copy-start(f32[512]{0:T(512)} %param.17) | copy-start | bytes 6148
  1.5 28.2 %all-to-all-start = ((f32[16,3,512]{2,1,0:T(4,128)}), f32[16,3,512]{2,1,0:T(4,128)S(1)}, u32[]{:S(2)}, u32[]{:S(2)}) async-start(f32[16,3,512]{2,1,0:T(4,128)} %broadcast_in_dim.7), calls=%async_computation | async-start | bytes 262144 | tf_op jit(solution)/shard_map/all_to_all | solution.py:359
  30.4 11.4 %all-to-all-start.1 = ((f32[8,19,4,128]{3,2,1,0:T(4,128)}), f32[8,19,4,128]{3,2,1,0:T(4,128)S(1)}, u32[]{:S(2)}, u32[]{:S(2)}) async-start(f32[8,19,4,128]{3,2,1,0:T(4,128)} %broadcast_in_dim.8), calls=%async_computation.1 | async-start | bytes 622592 | tf_op jit(solution)/shard_map/all_to_all | solution.py:358
  35.9 0.8 copy-start.1
  36.7 0.7 copy-start.12
  41.8 28.2 %all-to-all-start.2 = ((f32[4,1,128]{2,1,0:T(1,128)}), f32[4,1,128]{2,1,0:T(1,128)S(1)}, u32[]{:S(2)}, u32[]{:S(2)}) async-start(f32[4,1,128]{2,1,0:T(1,128)} %shard_map.129), calls=%async_computation.2 | async-start | bytes 4096 | tf_op jit(solution)/shard_map/all_to_all | solution.py:374
  47.1 0.7 copy-start.9
  49.0 0.7 copy-start.3
  49.7 0.7 copy-start.6
  50.4 0.7 copy-start.10
  70.0 0.7 copy-start.4
  70.7 0.7 copy-start.7

commit v2 on v1

--- a/solution.py
+++ b/solution.py
@@ -85,22 +85,46 @@
         ref[index, :, c * LANES : (c + 1) * LANES] = jnp.broadcast_to(lines[c : c + 1, :], (SUBS, LANES))
 
 
-def order_kernel(count_ref, lag_ref, order_ref):
+class Span:
+    def __init__(self, ref, start):
+        self.ref, self.start = ref, start
+
+    def __getitem__(self, index):
+        return self.ref[self.start + index]
+
+
+class Plan:
+    def __init__(self, ref):
+        pairs = (ref.shape[0] - STEPS - 3) // 4
+        self.near = Span(ref, 0)
+        self.upto = Span(ref, pairs - 1)
+        self.count = Span(ref, pairs + STEPS - 1)
+        self.target, self.source, self.lag = (Span(ref, pairs * i + STEPS) for i in (1, 2, 3))
+        self.place = Span(ref, 4 * pairs + STEPS)
+
+
+def write_plan(count_ref, target_ref, source_ref, lag_ref, adjacency_ref, plan_ref):
     pairs, count = lag_ref.shape[1], count_ref[0]
     lags = [jnp.where(p < count, lag_ref[0, p], 0) for p in range(pairs)]
     filled = jnp.int32(0)
     ends = []
     for lag in range(1, STEPS):
         for p in range(pairs):
-            order_ref[filled] = p
+            plan_ref[filled] = p
             filled = filled + (lags[p] == lag).astype(jnp.int32)
         ends.append(filled)
     for place, end in enumerate(ends + [count]):
-        order_ref[pairs + place] = end
-
-
-def two_at_a_time(count, pick, lists, tgt_ref, src_ref, works, steps, window_of, add):
-    target_ref, source_ref, lag_ref = lists
+        plan_ref[pairs + place] = end
+    for i, ref in enumerate((target_ref, source_ref, lag_ref)):
+        for p in range(pairs):
+            plan_ref[pairs * (i + 1) + STEPS + p] = ref[0, p]
+    region, regions = lax.axis_index("region"), lax.axis_size("region")
+    own = (region, lax.rem(region + adjacency_ref[0], regions), lax.axis_index("group"))
+    for i, value in enumerate(own):
+        plan_ref[4 * pairs + STEPS + i] = value
+
+
+def two_at_a_time(count, pick, plan, tgt_ref, src_ref, works, steps, window_of, add):
     nodes = src_ref.shape[2] * LANES
 
     def turn_fn(turn, carry):
@@ -108,7 +132,7 @@
         for side, (tb, geo, coef, acc) in enumerate(works):
             place = 2 * turn + side
             p = pick(jnp.minimum(place, count - 1))
-            tile, member, lag = target_ref[0, p], source_ref[0, p], lag_ref[0, p]
+            tile, member, lag = plan.target[p], plan.source[p], plan.lag[p]
             factor = jnp.where(place < count, 1.0 / 6.0, 0.0)
             spread_targets(tgt_ref, tile, tb)
             for k in range(3):
@@ -127,7 +151,7 @@
     lax.fori_loop(0, (count + 1) // 2, turn_fn, 0)
 
 
-def history_kernel(order_ref, target_ref, source_ref, lag_ref, tgt_ref, src_ref, out_ref, *work):
+def history_kernel(plan_ref, tgt_ref, src_ref, out_ref, *work):
     out_ref[...] = jnp.zeros_like(out_ref)
 
     def window_of(member, lag):
@@ -141,22 +165,21 @@
     def add(tile, rows):
         out_ref[tile] += rows
 
-    lists = (target_ref, source_ref, lag_ref)
-    two_at_a_time(
-        order_ref[target_ref.shape[1] + STEPS - 1], lambda p: p, lists, tgt_ref, src_ref, (work[:4], work[4:]), STEPS, window_of, add
-    )
-
-
-def near_kernel(order_ref, target_ref, source_ref, tgt_ref, src_ref, near_ref, *work):
+    plan = Plan(plan_ref)
+    two_at_a_time(plan.count[0], lambda p: p, plan, tgt_ref, src_ref, (work[:4], work[4:]), STEPS, window_of, add)
+
+
+def near_kernel(plan_ref, tgt_ref, src_ref, near_ref, *work):
     lines = src_ref.shape[2]
-    count = jnp.minimum(order_ref[target_ref.shape[1] + STEPS - 2], NEAR)
+    plan = Plan(plan_ref)
+    count = jnp.minimum(plan.upto[STEPS - 1], NEAR)
     spaces = (work[:2], work[2:])
 
     def turn_fn(turn, carry):
         for side, (tb, geo) in enumerate(spaces):
             slot = jnp.minimum(2 * turn + side, count - 1)
-            p = order_ref[slot]
-            tile, member = target_ref[0, p], source_ref[0, p]
+            p = plan.near[slot]
+            tile, member = plan.target[p], plan.source[p]
             spread_targets(tgt_ref, tile, tb)
             for k in range(3):
                 spread(geo, k, src_ref[member, k])
@@ -227,12 +250,13 @@
 
 
 def step_kernel(
-    step, order_ref, target_ref, source_ref, lag_ref, place_ref, near_ref, tgt_ref, src_ref, send_ref, own_ref, *refs
+    step, plan_ref, near_ref, tgt_ref, src_ref, send_ref, own_ref, *refs
 ):
     new_refs = refs[:step]
     out_ref, new = refs[step : step + 2]
     work = refs[step + 2 :]
-    region, group = place_ref[0], place_ref[2]
+    plan = Plan(plan_ref)
+    region, group = plan.place[0], plan.place[2]
     out_ref[...] = jnp.zeros_like(out_ref)
     new[...] = jnp.zeros_like(new)
     for j in range(step):
@@ -251,7 +275,7 @@
     def add(tile, rows):
         out_ref[region * tiles + tile] += rows
 
-    count = order_ref[target_ref.shape[1] + step - 1]
+    count = plan.upto[step]
     kept = jnp.minimum(count, NEAR)
 
     def turn_fn(turn, carry):
@@ -259,29 +283,39 @@
         for side in range(2):
             place = 2 * turn + side
             slot = jnp.minimum(place, kept - 1)
-            p = order_ref[slot]
-            share = near_sums(step, near_ref, slot, new, source_ref[0, p], lag_ref[0, p])
-            sums.append((target_ref[0, p], jnp.where(place < kept, share, 0.0)))
+            p = plan.near[slot]
+            share = near_sums(step, near_ref, slot, new, plan.source[p], plan.lag[p])
+            sums.append((plan.target[p], jnp.where(place < kept, share, 0.0)))
         for tile, share in sums:
             add(tile, share)
         return carry
 
     lax.fori_loop(0, (kept + 1) // 2, turn_fn, 0)
-    lists = (target_ref, source_ref, lag_ref)
     two_at_a_time(
-        count - kept, lambda p: order_ref[NEAR + p], lists, tgt_ref, src_ref, (work[:4], work[4:]), 1, window_of, add
+        count - kept, lambda p: plan.near[NEAR + p], plan, tgt_ref, src_ref, (work[:4], work[4:]), 1, window_of, add
     )
 
 
-def first_trace_kernel(send_ref, hist_ref, trace_ref):
-    trace = pick_trace(hist_ref[HIST - 1 : HIST, :], send_ref)
+def prepare_kernel(*refs):
+    write_plan(*refs[:5], refs[9])
+    positions, area, history, send = refs[5:9]
+    packed_ref, trace_ref = refs[10:]
+    rows = [positions[k : k + 1, :] for k in range(3)] + [area[...]]
+    rows += [history[k : k + 1, :] for k in range(FIRST_STORED, HIST)]
+    lines = packed_ref.shape[2]
+    for i, row in enumerate(rows):
+        block = jnp.concatenate([row[:, c * LANES : (c + 1) * LANES] for c in range(lines)], axis=0)
+        for member in range(packed_ref.shape[0]):
+            packed_ref[member, i] = block
+    trace = pick_trace(history[HIST - 1 : HIST, :], send)
     for r in range(trace_ref.shape[0]):
         trace_ref[r] = trace
 
 
-def density_kernel(step, place_ref, part_ref, recv_ref, gain_ref, inc_ref, self_ref, *refs):
+def density_kernel(step, plan_ref, part_ref, recv_ref, gain_ref, inc_ref, self_ref, *refs):
     nodes = inc_ref.shape[1]
-    region, partner, group = place_ref[0], place_ref[1], place_ref[2]
+    place = Plan(plan_ref).place
+    region, partner, group = place[0], place[1], place[2]
     last = step == STEPS - 1
     if step == 0:
         trace_ref, dens_ref, row_ref, past_ref = refs
@@ -346,31 +380,23 @@
     tiles = 2 * groups
     f32 = jnp.float32
     shape = jax.ShapeDtypeStruct
-    region = lax.axis_index("region")
-    place = jnp.stack([region, (region + adjacency[0]) % regions, lax.axis_index("group")]).astype(jnp.int32)
     self_row = self_weight.reshape(1, nodes)
-    lists = (pair_target, pair_source, pair_lag)
     line_rows = nodes // LANES
 
-    packed = jnp.concatenate([positions, area[None], history[FIRST_STORED:]], axis=0)
-    packed = packed.reshape(packed.shape[0], line_rows, LANES)
-    packed = jnp.broadcast_to(packed, (loops,) + packed.shape)
+    given = (pair_count, pair_target, pair_source, pair_lag, adjacency)
+    arrays = (positions, area.reshape(1, nodes), history, junc_send)
+    plan, packed, trace = pl.pallas_call(
+        prepare_kernel,
+        out_shape=(
+            shape((4 * pair_lag.shape[1] + STEPS + 3,), jnp.int32),
+            shape((loops, STORED_ROW + HIST - FIRST_STORED, line_rows, LANES), f32),
+            shape((regions, 1, jrows), f32),
+        ),
+        in_specs=[SMEM] * 5 + [VMEM] * 4,
+        out_specs=(SMEM, VMEM, VMEM),
+    )(*given, *arrays)
     sources = lax.all_to_all(packed, "loop", 0, 0, tiled=True)
     targets = lax.all_to_all(jnp.broadcast_to(positions, (groups, 3, nodes)), "group", 0, 0, tiled=True)
-    order = pl.pallas_call(
-        order_kernel,
-        out_shape=shape((pair_lag.shape[1] + STEPS,), jnp.int32),
-        in_specs=[SMEM] * 2,
-        out_specs=SMEM,
-        compiler_params=SMALL_GRANT,
-    )(pair_count, pair_lag)
-    trace = pl.pallas_call(
-        first_trace_kernel,
-        out_shape=shape((regions, 1, jrows), f32),
-        in_specs=[VMEM] * 2,
-        out_specs=VMEM,
-        compiler_params=SMALL_GRANT,
-    )(junc_send, history)
     traces = lax.all_to_all(trace, "region", 0, 0, tiled=True)
 
     def work(steps):
@@ -384,20 +410,20 @@
     partial_fields = pl.pallas_call(
         history_kernel,
         out_shape=shape((tiles, 2 * STEPS, LANES), f32),
-        in_specs=[SMEM] * 4 + [VMEM] * 2,
+        in_specs=[SMEM] + [VMEM] * 2,
         out_specs=VMEM,
         scratch_shapes=work(STEPS) * 2,
         compiler_params=PAIR_GRANT,
-    )(order, *lists, targets, sources)
-    order, place, partial_fields, traces = lax.optimization_barrier((order, place, partial_fields, traces))
+    )(plan, targets, sources)
+    plan, partial_fields, traces = lax.optimization_barrier((plan, partial_fields, traces))
     near = pl.pallas_call(
         near_kernel,
         out_shape=shape((NEAR, NEAR_COEFS, line_rows, half, LANES), f32),
-        in_specs=[SMEM] * 3 + [VMEM] * 2,
+        in_specs=[SMEM] + [VMEM] * 2,
         out_specs=VMEM,
         scratch_shapes=[pltpu.VMEM((3, half, LANES), f32), pltpu.VMEM((4, SUBS, nodes), f32)] * 2,
         compiler_params=NEAR_GRANT,
-    )(order, pair_target, pair_source, targets, sources)
+    )(plan, targets, sources)
     near, partial_fields = lax.optimization_barrier((near, partial_fields))
     parts = lax.all_to_all(partial_fields, "group", 0, 0, tiled=True)
 
@@ -409,13 +435,13 @@
             partial_fields = pl.pallas_call(
                 functools.partial(step_kernel, step),
                 out_shape=shape((regions * tiles, 2, LANES), f32),
-                in_specs=[SMEM] * 5 + [VMEM] * (5 + step),
+                in_specs=[SMEM] + [VMEM] * (5 + step),
                 out_specs=VMEM,
                 scratch_shapes=[pltpu.VMEM((loops, SUBS, line_rows, LANES), f32)] + work(1) * 2,
                 compiler_params=NEAR_GRANT,
-            )(order, *lists, place, near, targets, sources, junc_send, rows[-1], *gathered)
+            )(plan, near, targets, sources, junc_send, rows[-1], *gathered)
             parts = lax.all_to_all(partial_fields, ("region", "group"), 0, 0, tiled=True)
-        operands = [place, parts, junc_recv, junc_gain, incident, self_row]
+        operands = [plan, parts, junc_recv, junc_gain, incident, self_row]
         if step == 0:
             operands += [traces]
             out_shape = [dens_shape, row_shape, shape((2 * 2 * STEPS, LANES), f32)]

time: 179 us -> 173 us (0.966)
  blocking collectives: 95.6 us -> 107 us
  local copies, waits for them, and re-layouts: 9.02 us -> 2.65 us
  starting transfers between devices: 25 us -> 20.2 us
  waiting for transfers between devices: 14.1 us -> 9.43 us
    all_to_all x0 -> x1, blocking collectives: none -> 11.4 us  [body(): sources = lax.all_to_all(packed, 'loop', 0, 0, tiled=True)]
    all_to_all x1 -> x0, starting transfers between devices: 4.83 us -> none  [body(): sources = lax.all_to_all(packed, 'loop', 0, 0, tiled=True)]
    unnamed x32 -> x16, local copies, waits for them, and re-layouts: 5.36 us -> 1.24 us
    all_to_all x1 -> x0, waiting for transfers between devices: 3.75 us -> none  [body(): sources = lax.all_to_all(packed, 'loop', 0, 0, tiled=True)]
  transfers between devices with their start and end apart: 3 -> 2, of which waited for: 2 -> 1; matrix products, arithmetic and copies ran while one was open for 1% -> 0% of each run, Pallas kernels for 12% -> 12%
where the time goes in v2:
time: 173 us; the launch traced here: 172 us
  blocking collectives  107 us (62%)
  Pallas kernels  31.6 us (18%)
  starting transfers between devices  20.2 us (12%)
  waiting for transfers between devices  9.43 us (5%)
  local copies, waits for them, and re-layouts  2.65 us (2%)
    all_to_all x3, blocking collectives, body(): lax.all_to_all(partial_fields, ('region', 'group'), 0, 0, tiled=True)  52.4 us
    all_to_all x3, blocking collectives, body(): gathered.append(lax.all_to_all(results[0], 'loop', 0, 0, tiled=True))  26 us
    pallas_call x1, Pallas kernels, body(): pl.pallas_call(history_kernel, out_shape=shape((tiles, 2 * STEPS, LANES),...  19 us
    all_to_all x1, blocking collectives, body(): parts = lax.all_to_all(partial_fields, 'group', 0, 0, tiled=True)  17.1 us
    all_to_all x1, starting transfers between devices, body(): lax.all_to_all(jnp.broadcast_to(positions, (groups, 3, nodes)), 'group',...  15.6 us
    all_to_all x1, blocking collectives, body(): sources = lax.all_to_all(packed, 'loop', 0, 0, tiled=True)  11.4 us
    all_to_all x1, waiting for transfers between devices, body(): lax.all_to_all(jnp.broadcast_to(positions, (groups, 3, nodes)), 'group',...  9.43 us
    all_to_all x1, starting transfers between devices, body(): traces = lax.all_to_all(trace, 'region', 0, 0, tiled=True)  4.5 us
  transfers between devices with their start and end apart: 2, of which 1 were waited for; matrix products, arithmetic and copies ran while one was open for 0% of the time, Pallas kernels for 12%

profile of v2, /device:TPU:2, one launch (start us, length us, event | category | flops | bytes accessed | tf_op | source)
XLA Modules:
  0.0 172.2 jit_solution(4564972338012255674)
XLA Ops:
  0.0 0.0 copy-start.5
  0.0 0.0 copy-start.7
  0.0 0.0 copy-start.6
  0.0 0.0 copy-start
  0.0 0.0 copy-start.4
  0.0 1.4 broadcast_in_dim.3
  1.4 15.6 %all-to-all-start = ((f32[16,3,512]{2,1,0:T(4,128)}), f32[16,3,512]{2,1,0:T(4,128)S(1)}, u32[]{:S(2)}, u32[]{:S(2)}) async-start(f32[16,3,512]{2,1,0:T(4,128)} %broadcast_in_dim.3), calls=%async_computation | async-start | bytes 262144 | tf_op jit(solution)/shard_map/all_to_all | solution.py:399
  18.4 1.8 %shard_map.127 = (s32[103]{0:T(128)}, f32[8,19,4,128]{3,2,1,0:T(4,128)}, f32[4,1,128]{2,1,0:T(1,128)}) custom-call(s32[1]{0:T(128)S(6)} %copy.14.refs_0_, s32[1,24]{1,0:T(1,128)} %refs_1_.1, s32[1,24]{1,0:T(1,128)} %refs_2_.1, s32[1,24]{1,0:T(1,128)} %refs_3_.1, s32[1]{0:T(128)S(6)} %copy.15.refs_4_, f32[3,512]{1,0:T(4,128)} %refs_5_.1, f32[1,512]{1,0:T(1,128)} %bitcast.6, ...), custom_call_target="tpu_custom_call" | custom-call | tf_op jit(solution)/shard_map/pallas_call | solution.py:388
  20.2 0.0 copy-start.3
  20.2 9.4 %all-to-all-done.tgt_ref = f32[16,3,512]{2,1,0:T(4,128)S(1)} async-done(((f32[16,3,512]{2,1,0:T(4,128)}), f32[16,3,512]{2,1,0:T(4,128)S(1)}, u32[]{:S(2)}, u32[]{:S(2)}) %all-to-all-start) | async-done | bytes 98336 | tf_op jit(solution)/shard_map/all_to_all | solution.py:399
  29.6 11.4 %all_to_all.50.src_ref = f32[8,19,4,128]{3,2,1,0:T(4,128)S(1)} all-to-all(f32[8,19,4,128]{3,2,1,0:T(4,128)} %get-tuple-element.21), channel_id=1, replica_groups=mesh['region'=4,'group'=16,'loop'=8] {'loop'}, dimensions={0} | all-to-all | bytes 622592 | tf_op jit(solution)/shard_map/all_to_all | solution.py:398
  41.0 4.5 %all-to-all-start.2 = ((f32[4,1,128]{2,1,0:T(1,128)}), f32[4,1,128]{2,1,0:T(1,128)S(1)}, u32[]{:S(2)}, u32[]{:S(2)}) async-start(f32[4,1,128]{2,1,0:T(1,128)} %get-tuple-element.22), calls=%async_computation.2 | async-start | bytes 4096 | tf_op jit(solution)/shard_map/all_to_all | solution.py:400
  45.5 0.0 copy-start.1
  45.5 0.6 copy-done.1
  46.2 19.0 %shard_map.128 = f32[32,8,128]{2,1,0:T(8,128)S(1)} custom-call(s32[103]{0:T(128)S(1)} %copy-done.1, f32[16,3,512]{2,1,0:T(4,128)S(1)} %all-to-all-done.tgt_ref, f32[8,19,4,128]{3,2,1,0:T(4,128)S(1)} %all_to_all.50.src_ref), custom_call_target="tpu_custom_call" | custom-call | tf_op jit(solution)/shard_map/pallas_call | solution.py:410
  65.2 0.0 all-to-all-done.2.refs_0_
  65.2 0.0 copy-start.2
  65.2 0.6 copy-done.2
  65.8 3.6 %shard_map.129.near_ref = f32[12,3,4,256,128]{4,3,2,1,0:T(8,128)S(1)} custom-call(s32[103]{0:T(128)S(1)} %copy-done.2, f32[16,3,512]{2,1,0:T(4,128)S(1)} %all-to-all-done.tgt_ref, f32[8,19,4,128]{3,2,1,0:T(4,128)S(1)} %all_to_all.50.src_ref), custom_call_target="tpu_custom_call" | custom-call | tf_op jit(solution)/shard_map/pallas_call | solution.py:419
  69.4 17.1 %all_to_all.51.part_ref = f32[32,8,128]{2,1,0:T(8,128)S(1)} all-to-all(f32[32,8,128]{2,1,0:T(8,128)S(1)} %shard_map.128), channel_id=1, replica_groups=mesh['region'=4,'group'=16,'loop'=8] {'group'}, dimensions={0} | all-to-all | bytes 262144 | tf_op jit(solution)/shard_map/all_to_all | solution.py:428
  86.4 0.0 copy-done.7
  86.4 0.0 copy-done.6
  86.4 0.0 copy-done
  86.4 0.0 copy-done.4
  86.4 0.7 shard_map.130
  87.2 10.7 %all_to_all.52.refs_0_ = f32[8,4,128]{2,1,0:T(4,128)S(1)} all-to-all(f32[8,4,128]{2,1,0:T(4,128)S(1)} %get-tuple-element.29), channel_id=1, replica_groups=mesh['region'=4,'group'=16,'loop'=8] {'loop'}, dimensions={0} | all-to-all | bytes 32768 | tf_op jit(solution)/shard_map/all_to_all | solution.py:465
  97.9 0.0 copy-done.5
  97.9 0.0 copy-done.3
  97.9 0.9 shard_map.131
  98.8 19.0 %all_to_all.53.part_ref = f32[128,2,128]{2,1,0:T(2,128)S(1)} all-to-all(f32[128,2,128]{2,1,0:T(2,128)S(1)} %shard_map.131), channel_id=1, replica_groups=mesh['region'=4,'group'=16,'loop'=8] {'region','group'}, dimensions={0} | all-to-all | bytes 262144 | tf_op jit(solution)/shard_map/all_to_all | solution.py:443
  117.8 0.7 shard_map.132
  118.5 7.7 %all_to_all.54.refs_1_ = f32[8,4,128]{2,1,0:T(4,128)S(1)} all-to-all(f32[8,4,128]{2,1,0:T(4,128)S(1)} %get-tuple-element.32), channel_id=1, replica_groups=mesh['region'=4,'group'=16,'loop'=8] {'loop'}, dimensions={0} | all-to-all | bytes 32768 | tf_op jit(solution)/shard_map/all_to_all | solution.py:465
  126.2 1.2 shard_map.133
  127.4 16.5 %all_to_all.55.part_ref = f32[128,2,128]{2,1,0:T(2,128)S(1)} all-to-all(f32[128,2,128]{2,1,0:T(2,128)S(1)} %shard_map.133), channel_id=1, replica_groups=mesh['region'=4,'group'=16,'loop'=8] {'region','group'}, dimensions={0} | all-to-all | bytes 262144 | tf_op jit(solution)/shard_map/all_to_all | solution.py:443
  143.9 0.7 shard_map.134
  144.6 7.6 %all_to_all.56.refs_2_ = f32[8,4,128]{2,1,0:T(4,128)S(1)} all-to-all(f32[8,4,128]{2,1,0:T(4,128)S(1)} %get-tuple-element.34), channel_id=1, replica_groups=mesh['region'=4,'group'=16,'loop'=8] {'loop'}, dimensions={0} | all-to-all | bytes 32768 | tf_op jit(solution)/shard_map/all_to_all | solution.py:465
  152.2 1.7 shard_map.135
  153.9 17.0 %all_to_all.57.part_ref = f32[128,2,128]{2,1,0:T(2,128)S(1)} all-to-all(f32[128,2,128]{2,1,0:T(2,128)S(1)} %shard_map.135), channel_id=1, replica_groups=mesh['region'=4,'group'=16,'loop'=8] {'region','group'}, dimensions={0} | all-to-all | bytes 262144 | tf_op jit(solution)/shard_map/all_to_all | solution.py:443
  170.9 1.3 shard_map.136
Async XLA Ops:
  0.0 97.9 %copy-start.5 = (s32[1,128]{1,0:T(1,128)S(1)}, s32[1,128]{1,0:T(1,128)}, u32[]{:S(2)}) copy-start(s32[1,128]{1,0:T(1,128)} %send_ref.5) | copy-start | bytes 1540
  0.0 86.4 %copy-start.7 = (f32[1,128]{1,0:T(1,128)S(1)}, f32[1,128]{1,0:T(1,128)}, u32[]{:S(2)}) copy-start(f32[1,128]{1,0:T(1,128)} %gain_ref.7) | copy-start | bytes 1540
  0.0 86.4 %copy-start.6 = (s32[1,128]{1,0:T(1,128)S(1)}, s32[1,128]{1,0:T(1,128)}, u32[]{:S(2)}) copy-start(s32[1,128]{1,0:T(1,128)} %recv_ref.7) | copy-start | bytes 1540
  0.0 86.4 %copy-start = (f32[4,512]{1,0:T(4,128)S(1)}, f32[4,512]{1,0:T(4,128)}, u32[]{:S(2)}) copy-start(f32[4,512]{1,0:T(4,128)} %inc_ref.7) | copy-start | bytes 24580
  0.0 86.4 %copy-start.4 = (f32[512]{0:T(512)S(1)}, f32[512]{0:T(512)}, u32[]{:S(2)}) copy-start(f32[512]{0:T(512)} %param.17) | copy-start | bytes 6148
  1.4 28.2 %all-to-all-start = ((f32[16,3,512]{2,1,0:T(4,128)}), f32[16,3,512]{2,1,0:T(4,128)S(1)}, u32[]{:S(2)}, u32[]{:S(2)}) async-start(f32[16,3,512]{2,1,0:T(4,128)} %broadcast_in_dim.3), calls=%async_computation | async-start | bytes 262144 | tf_op jit(solution)/shard_map/all_to_all | solution.py:399
  20.2 77.7 %copy-start.3 = (s32[103]{0:T(128)S(1)}, s32[103]{0:T(128)}, u32[]{:S(2)}) copy-start(s32[103]{0:T(128)} %get-tuple-element.23.plan_ref) | copy-start | bytes 1240
  41.0 24.1 %all-to-all-start.2 = ((f32[4,1,128]{2,1,0:T(1,128)}), f32[4,1,128]{2,1,0:T(1,128)S(1)}, u32[]{:S(2)}, u32[]{:S(2)}) async-start(f32[4,1,128]{2,1,0:T(1,128)} %get-tuple-element.22), calls=%async_computation.2 | async-start | bytes 4096 | tf_op jit(solution)/shard_map/all_to_all | solution.py:400
  45.5 0.6 copy-start.1
  65.2 0.6 copy-start.2

commit v3 on v2

--- a/solution.py
+++ b/solution.py
@@ -175,7 +175,7 @@
     count = jnp.minimum(plan.upto[STEPS - 1], NEAR)
     spaces = (work[:2], work[2:])
 
-    def turn_fn(turn, carry):
+    def run(turn, kinds):
         for side, (tb, geo) in enumerate(spaces):
             slot = jnp.minimum(2 * turn + side, count - 1)
             p = plan.near[slot]
@@ -199,12 +199,25 @@
                     u = 1.0 / (1.0 + dist_sq)
                     square = u * u
                     cube = square * u
-                    near_ref[slot, 0, c, rows, :] = weight * cube
-                    near_ref[slot, 1, c, rows, :] = weight * (1.0 + 3.0 * (u + square - cube))
-                    near_ref[slot, 2, c, rows, :] = weight * (4.0 + 3.0 * (cube - 2.0 * square))
+                    values = [
+                        weight * cube,
+                        weight * (1.0 + 3.0 * (u + square - cube)) if kinds > 1 else None,
+                        weight * (4.0 + 3.0 * (cube - 2.0 * square)) if kinds > 2 else None,
+                    ]
+                    for kind, value in enumerate(values):
+                        near_ref[slot, kind, c, rows, :] = jnp.zeros_like(cube) if value is None else value
                 return carry
 
             lax.fori_loop(0, tb.shape[1] // SUBS, block_fn, 0, unroll=tb.shape[1] // SUBS)
+
+    def turn_fn(turn, carry):
+        lead = plan.lag[plan.near[2 * turn]]
+        for kinds in range(1, STEPS):
+
+            @pl.when(lead == STEPS - kinds)
+            def _(kinds=kinds):
+                run(turn, kinds)
+
         return carry
 
     lax.fori_loop(0, (count + 1) // 2, turn_fn, 0)

time: 173 us -> 173 us (level)
  no operation moved by 1% of the time
where the time goes in v3:
time: 173 us; the launch traced here: 172 us
  blocking collectives  107 us (62%)
  Pallas kernels  31.3 us (18%)
  starting transfers between devices  20.2 us (12%)
  waiting for transfers between devices  9.43 us (5%)
  local copies, waits for them, and re-layouts  2.65 us (2%)
    all_to_all x3, blocking collectives, body(): lax.all_to_all(partial_fields, ('region', 'group'), 0, 0, tiled=True)  52.8 us
    all_to_all x3, blocking collectives, body(): gathered.append(lax.all_to_all(results[0], 'loop', 0, 0, tiled=True))  25.6 us
    pallas_call x1, Pallas kernels, body(): pl.pallas_call(history_kernel, out_shape=shape((tiles, 2 * STEPS, LANES),...  19 us
    all_to_all x1, blocking collectives, body(): parts = lax.all_to_all(partial_fields, 'group', 0, 0, tiled=True)  17 us
    all_to_all x1, starting transfers between devices, body(): lax.all_to_all(jnp.broadcast_to(positions, (groups, 3, nodes)), 'group',...  15.6 us
    all_to_all x1, blocking collectives, body(): sources = lax.all_to_all(packed, 'loop', 0, 0, tiled=True)  11.4 us
    all_to_all x1, waiting for transfers between devices, body(): lax.all_to_all(jnp.broadcast_to(positions, (groups, 3, nodes)), 'group',...  9.43 us
    all_to_all x1, starting transfers between devices, body(): traces = lax.all_to_all(trace, 'region', 0, 0, tiled=True)  4.5 us
  transfers between devices with their start and end apart: 2, of which 1 were waited for; matrix products, arithmetic and copies ran while one was open for 0% of the time, Pallas kernels for 12%

profile of v3, /device:TPU:2, one launch (start us, length us, event | category | flops | bytes accessed | tf_op | source)
XLA Modules:
  0.0 171.8 jit_solution(437103149996103588)
XLA Ops:
  0.0 0.0 copy-start.5
  0.0 0.0 copy-start.7
  0.0 0.0 copy-start.6
  0.0 0.0 copy-start
  0.0 0.0 copy-start.4
  0.0 1.4 broadcast_in_dim.3
  1.4 15.6 %all-to-all-start = ((f32[16,3,512]{2,1,0:T(4,128)}), f32[16,3,512]{2,1,0:T(4,128)S(1)}, u32[]{:S(2)}, u32[]{:S(2)}) async-start(f32[16,3,512]{2,1,0:T(4,128)} %broadcast_in_dim.3), calls=%async_computation | async-start | bytes 262144 | tf_op jit(solution)/shard_map/all_to_all | solution.py:412
  18.4 1.8 %shard_map.127 = (s32[103]{0:T(128)}, f32[8,19,4,128]{3,2,1,0:T(4,128)}, f32[4,1,128]{2,1,0:T(1,128)}) custom-call(s32[1]{0:T(128)S(6)} %copy.14.refs_0_, s32[1,24]{1,0:T(1,128)} %refs_1_.1, s32[1,24]{1,0:T(1,128)} %refs_2_.1, s32[1,24]{1,0:T(1,128)} %refs_3_.1, s32[1]{0:T(128)S(6)} %copy.15.refs_4_, f32[3,512]{1,0:T(4,128)} %refs_5_.1, f32[1,512]{1,0:T(1,128)} %bitcast.6, ...), custom_call_target="tpu_custom_call" | custom-call | tf_op jit(solution)/shard_map/pallas_call | solution.py:401
  20.2 0.0 copy-start.3
  20.2 9.4 %all-to-all-done.tgt_ref = f32[16,3,512]{2,1,0:T(4,128)S(1)} async-done(((f32[16,3,512]{2,1,0:T(4,128)}), f32[16,3,512]{2,1,0:T(4,128)S(1)}, u32[]{:S(2)}, u32[]{:S(2)}) %all-to-all-start) | async-done | bytes 98336 | tf_op jit(solution)/shard_map/all_to_all | solution.py:412
  29.6 11.4 %all_to_all.50.src_ref = f32[8,19,4,128]{3,2,1,0:T(4,128)S(1)} all-to-all(f32[8,19,4,128]{3,2,1,0:T(4,128)} %get-tuple-element.21), channel_id=1, replica_groups=mesh['region'=4,'group'=16,'loop'=8] {'loop'}, dimensions={0} | all-to-all | bytes 622592 | tf_op jit(solution)/shard_map/all_to_all | solution.py:411
  41.0 4.5 %all-to-all-start.2 = ((f32[4,1,128]{2,1,0:T(1,128)}), f32[4,1,128]{2,1,0:T(1,128)S(1)}, u32[]{:S(2)}, u32[]{:S(2)}) async-start(f32[4,1,128]{2,1,0:T(1,128)} %get-tuple-element.22), calls=%async_computation.2 | async-start | bytes 4096 | tf_op jit(solution)/shard_map/all_to_all | solution.py:413
  45.5 0.0 copy-start.1
  45.5 0.6 copy-done.1
  46.2 19.0 %shard_map.128 = f32[32,8,128]{2,1,0:T(8,128)S(1)} custom-call(s32[103]{0:T(128)S(1)} %copy-done.1, f32[16,3,512]{2,1,0:T(4,128)S(1)} %all-to-all-done.tgt_ref, f32[8,19,4,128]{3,2,1,0:T(4,128)S(1)} %all_to_all.50.src_ref), custom_call_target="tpu_custom_call" | custom-call | tf_op jit(solution)/shard_map/pallas_call | solution.py:423
  65.2 0.0 all-to-all-done.2.refs_0_
  65.2 0.0 copy-start.2
  65.2 0.6 copy-done.2
  65.8 3.3 %shard_map.129.near_ref = f32[12,3,4,256,128]{4,3,2,1,0:T(8,128)S(1)} custom-call(s32[103]{0:T(128)S(1)} %copy-done.2, f32[16,3,512]{2,1,0:T(4,128)S(1)} %all-to-all-done.tgt_ref, f32[8,19,4,128]{3,2,1,0:T(4,128)S(1)} %all_to_all.50.src_ref), custom_call_target="tpu_custom_call" | custom-call | tf_op jit(solution)/shard_map/pallas_call | solution.py:432
  69.1 17.0 %all_to_all.51.part_ref = f32[32,8,128]{2,1,0:T(8,128)S(1)} all-to-all(f32[32,8,128]{2,1,0:T(8,128)S(1)} %shard_map.128), channel_id=1, replica_groups=mesh['region'=4,'group'=16,'loop'=8] {'group'}, dimensions={0} | all-to-all | bytes 262144 | tf_op jit(solution)/shard_map/all_to_all | solution.py:441
  86.1 0.0 copy-done.7
  86.1 0.0 copy-done.6
  86.1 0.0 copy-done
  86.1 0.0 copy-done.4
  86.1 0.7 shard_map.130
  86.8 10.4 %all_to_all.52.refs_0_ = f32[8,4,128]{2,1,0:T(4,128)S(1)} all-to-all(f32[8,4,128]{2,1,0:T(4,128)S(1)} %get-tuple-element.29), channel_id=1, replica_groups=mesh['region'=4,'group'=16,'loop'=8] {'loop'}, dimensions={0} | all-to-all | bytes 32768 | tf_op jit(solution)/shard_map/all_to_all | solution.py:478
  97.2 0.0 copy-done.5
  97.2 0.0 copy-done.3
  97.2 0.9 shard_map.131
  98.1 19.4 %all_to_all.53.part_ref = f32[128,2,128]{2,1,0:T(2,128)S(1)} all-to-all(f32[128,2,128]{2,1,0:T(2,128)S(1)} %shard_map.131), channel_id=1, replica_groups=mesh['region'=4,'group'=16,'loop'=8] {'region','group'}, dimensions={0} | all-to-all | bytes 262144 | tf_op jit(solution)/shard_map/all_to_all | solution.py:456
  117.5 0.7 shard_map.132
  118.2 7.6 %all_to_all.54.refs_1_ = f32[8,4,128]{2,1,0:T(4,128)S(1)} all-to-all(f32[8,4,128]{2,1,0:T(4,128)S(1)} %get-tuple-element.32), channel_id=1, replica_groups=mesh['region'=4,'group'=16,'loop'=8] {'loop'}, dimensions={0} | all-to-all | bytes 32768 | tf_op jit(solution)/shard_map/all_to_all | solution.py:478
  125.8 1.2 shard_map.133
  127.0 16.5 %all_to_all.55.part_ref = f32[128,2,128]{2,1,0:T(2,128)S(1)} all-to-all(f32[128,2,128]{2,1,0:T(2,128)S(1)} %shard_map.133), channel_id=1, replica_groups=mesh['region'=4,'group'=16,'loop'=8] {'region','group'}, dimensions={0} | all-to-all | bytes 262144 | tf_op jit(solution)/shard_map/all_to_all | solution.py:456
  143.5 0.7 shard_map.134
  144.3 7.6 %all_to_all.56.refs_2_ = f32[8,4,128]{2,1,0:T(4,128)S(1)} all-to-all(f32[8,4,128]{2,1,0:T(4,128)S(1)} %get-tuple-element.34), channel_id=1, replica_groups=mesh['region'=4,'group'=16,'loop'=8] {'loop'}, dimensions={0} | all-to-all | bytes 32768 | tf_op jit(solution)/shard_map/all_to_all | solution.py:478
  151.9 1.7 shard_map.135
  153.6 17.0 %all_to_all.57.part_ref = f32[128,2,128]{2,1,0:T(2,128)S(1)} all-to-all(f32[128,2,128]{2,1,0:T(2,128)S(1)} %shard_map.135), channel_id=1, replica_groups=mesh['region'=4,'group'=16,'loop'=8] {'region','group'}, dimensions={0} | all-to-all | bytes 262144 | tf_op jit(solution)/shard_map/all_to_all | solution.py:456
  170.5 1.3 shard_map.136
Async XLA Ops:
  0.0 97.2 %copy-start.5 = (s32[1,128]{1,0:T(1,128)S(1)}, s32[1,128]{1,0:T(1,128)}, u32[]{:S(2)}) copy-start(s32[1,128]{1,0:T(1,128)} %send_ref.5) | copy-start | bytes 1540
  0.0 86.1 %copy-start.7 = (f32[1,128]{1,0:T(1,128)S(1)}, f32[1,128]{1,0:T(1,128)}, u32[]{:S(2)}) copy-start(f32[1,128]{1,0:T(1,128)} %gain_ref.7) | copy-start | bytes 1540
  0.0 86.1 %copy-start.6 = (s32[1,128]{1,0:T(1,128)S(1)}, s32[1,128]{1,0:T(1,128)}, u32[]{:S(2)}) copy-start(s32[1,128]{1,0:T(1,128)} %recv_ref.7) | copy-start | bytes 1540
  0.0 86.1 %copy-start = (f32[4,512]{1,0:T(4,128)S(1)}, f32[4,512]{1,0:T(4,128)}, u32[]{:S(2)}) copy-start(f32[4,512]{1,0:T(4,128)} %inc_ref.7) | copy-start | bytes 24580
  0.0 86.1 %copy-start.4 = (f32[512]{0:T(512)S(1)}, f32[512]{0:T(512)}, u32[]{:S(2)}) copy-start(f32[512]{0:T(512)} %param.17) | copy-start | bytes 6148
  1.4 28.2 %all-to-all-start = ((f32[16,3,512]{2,1,0:T(4,128)}), f32[16,3,512]{2,1,0:T(4,128)S(1)}, u32[]{:S(2)}, u32[]{:S(2)}) async-start(f32[16,3,512]{2,1,0:T(4,128)} %broadcast_in_dim.3), calls=%async_computation | async-start | bytes 262144 | tf_op jit(solution)/shard_map/all_to_all | solution.py:412
  20.2 77.0 %copy-start.3 = (s32[103]{0:T(128)S(1)}, s32[103]{0:T(128)}, u32[]{:S(2)}) copy-start(s32[103]{0:T(128)} %get-tuple-element.23.plan_ref) | copy-start | bytes 1240
  41.0 24.1 %all-to-all-start.2 = ((f32[4,1,128]{2,1,0:T(1,128)}), f32[4,1,128]{2,1,0:T(1,128)S(1)}, u32[]{:S(2)}, u32[]{:S(2)}) async-start(f32[4,1,128]{2,1,0:T(1,128)} %get-tuple-element.22), calls=%async_computation.2 | async-start | bytes 4096 | tf_op jit(solution)/shard_map/all_to_all | solution.py:413
  45.5 0.6 copy-start.1
  65.2 0.6 copy-start.2
